TPU v7x, 512 devices: a whole 4x4x16 slice. The times are simulated.
512 devices in a mesh: dp: 64 (over z, x_hi, core), mp: 8 (over x_lo, y).
Axes of the slice: x: 4 (x_hi: 2, x_lo: 2; x = x_hi * 2 + x_lo), y: 4, z: 16, core: 2. Of those that a mesh axis runs over, the one named last changes fastest.
Arguments:
- normed_input_rows: bfloat16 [24576, 8192], P('dp', 'mp'), may hold values from -6 to 6
- frozen_queries: bfloat16 [24576, 8192], P('dp', 'mp'), may hold values from -6 to 6
- frozen_keys: bfloat16 [24576, 1024], P('dp', 'mp'), may hold values from -6 to 6
- frozen_values: bfloat16 [24576, 1024], P('dp', 'mp'), may hold values from -6 to 6
- attention_output_gradient: bfloat16 [24576, 8192], P('dp', 'mp'), may hold values from -1.1953125 to 1.1953125
- adapter_down_weight: float32 [64, 8192, 192], P(None, ('mp', 'dp')), may hold values from -0.0625 to 0.0625
- adapter_up_query: float32 [64, 64, 8192], P(None, 'dp', 'mp'), may hold values from -0.75 to 0.75
- adapter_up_key_value: float32 [64, 64, 8, 256], P(None, 'dp', 'mp'), may hold values from -0.75 to 0.75
- document_numbers: int32 [24576], P('dp'), may hold values from 0 to 1535, as said below
- block_tenant_slot: int32 [192], P('dp'), may hold values from 0 to 1, as said below
- shard_tenant_table: int32 [64, 2], replicated, may hold values from 0 to 63, as said below
Outputs:
- grad_down: float32 [64, 8192, 192], P(None, ('mp', 'dp'))
- grad_upq: float32 [64, 64, 8192], P(None, 'dp', 'mp')
- grad_upkv: float32 [64, 64, 8, 256], P(None, 'dp', 'mp')
Inputs may be any that keep to these rules, and one draw needn't show every extreme that they name: `document_numbers`: document numbers never fall along the rows; a document starts only at a multiple of 16 rows, always at the first row of each index of dp, at the last 16 rows of all, and wherever the slot of a block changes; a document's number is its first row divided by 16. `block_tenant_slot`: the 3 blocks of each index of dp name slots in an order that never falls, and every one of the 2 slots is named. `shard_tenant_table`: each row holds 2 distinct tenants.
All inputs are finite; a program needn't handle non-finite values.
Results may differ from a plain program's by a relative error of at most 0.012.
The roundings to bfloat16 on the way count: a program that leaves them out, or rounds other values in their place, can miss the bound.
Values sent between devices are 32-bit elements; how exact they have to be, the bound alone decides.
A program may use at most 64 MiB of HBM per device.

v0:
```python
import jax
import jax.numpy as jnp
from jax import lax
from jax.sharding import PartitionSpec as P

ADAPTER_SCALE = 0.5
MASKED = -1e30
PRECISION_HIGH = lax.Precision.HIGHEST


def attention_grads(query_row_block, key_row_block, value_row_block, upstream, doc_row):
    row_total = query_row_block.shape[0]
    kv_heads = key_row_block.shape[1]
    groups = query_row_block.shape[1] // kv_heads
    head_size = query_row_block.shape[2]
    query_g = query_row_block.reshape(row_total, kv_heads, groups, head_size)
    upstream_g = upstream.reshape(row_total, kv_heads, groups, head_size)
    inverse = 1.0 / head_size**0.5
    scores = (
        jnp.einsum("qkgd,jkd->kgqj", query_g, key_row_block, preferred_element_type=jnp.float32)
        * inverse
    )
    position = jnp.arange(row_total, dtype=jnp.int32)
    allowed = (doc_row[:, None] == doc_row[None, :]) & (position[:, None] >= position[None, :])
    scores = jnp.where(allowed, scores, MASKED)
    row_top = jnp.max(scores, axis=-1, keepdims=True)
    weights = jnp.exp(scores - row_top)
    attn_probs = weights / jnp.sum(weights, axis=-1, keepdims=True)
    probs_low = attn_probs.astype(jnp.bfloat16)
    grad_probs = jnp.einsum(
        "qkgd,jkd->kgqj", upstream_g, value_row_block, preferred_element_type=jnp.float32
    )
    row_inner = jnp.sum(attn_probs * grad_probs, axis=-1, keepdims=True)
    grad_scores = (attn_probs * (grad_probs - row_inner) * inverse).astype(jnp.bfloat16)
    grad_query = jnp.einsum(
        "kgqj,jkd->qkgd", grad_scores, key_row_block, preferred_element_type=jnp.float32
    ).reshape(row_total, -1)
    key_gradient = jnp.einsum(
        "kgqj,qkgd->jkd", grad_scores, query_g, preferred_element_type=jnp.float32
    ).reshape(row_total, -1)
    value_gradient = jnp.einsum(
        "kgqj,qkgd->jkd", probs_low, upstream_g, preferred_element_type=jnp.float32
    ).reshape(row_total, -1)
    return (grad_query, key_gradient, value_gradient)


def adapted(frozen_rows, low_part, panel_cols):
    extra_term = jnp.einsum("brk,bkc->brc", low_part, panel_cols, precision=PRECISION_HIGH)
    extra_term = extra_term.reshape(frozen_rows.shape[0], -1)
    return (frozen_rows.astype(jnp.float32) + ADAPTER_SCALE * extra_term).astype(jnp.bfloat16)


def on_device(
    normed_input_rows,
    frozen_queries,
    frozen_keys,
    frozen_values,
    attention_output_gradient,
    adapter_down_weight,
    adapter_up_query,
    adapter_up_key_value,
    document_numbers,
    block_tenant_slot,
    shard_tenant_table,
):
    row_count = normed_input_rows.shape[0]
    block_count = block_tenant_slot.shape[0]
    block_rows = row_count // block_count
    dp_count = lax.axis_size("dp")
    count_of_tenants = adapter_down_weight.shape[0]
    desired_result = shard_tenant_table.reshape(-1)
    down_panels, upq_panels, upkv_panels = (
        lax.all_to_all(
            adapter_down_weight[desired_result], "dp", split_axis=0, concat_axis=1, tiled=True
        ),
        lax.all_to_all(
            adapter_up_query[desired_result], "dp", split_axis=0, concat_axis=1, tiled=True
        ),
        lax.all_to_all(
            adapter_up_key_value[desired_result], "dp", split_axis=0, concat_axis=1, tiled=True
        ),
    )
    adapter_rank = down_panels.shape[2] // 3
    row_blocks = normed_input_rows.reshape(block_count, block_rows, -1).astype(jnp.float32)
    partial_down = jnp.einsum(
        "bri,bij->brj", row_blocks, down_panels[block_tenant_slot], precision=PRECISION_HIGH
    )
    lowrank = lax.psum(partial_down.reshape(row_count, 3 * adapter_rank), "mp")
    head_size = upkv_panels.shape[3] // 2
    kv_heads = upkv_panels.shape[2]
    query_heads = frozen_queries.shape[1] // head_size
    low_blocks = lowrank.reshape(block_count, block_rows, 3, adapter_rank)
    upq_blocks = upq_panels[block_tenant_slot]
    upkv_blocks = upkv_panels[block_tenant_slot]
    upk_blocks = upkv_blocks[..., :head_size].reshape(
        block_count, adapter_rank, kv_heads * head_size
    )
    upv_blocks = upkv_blocks[..., head_size:].reshape(
        block_count, adapter_rank, kv_heads * head_size
    )
    query_row_block = adapted(frozen_queries, low_blocks[:, :, 0], upq_blocks)
    key_row_block = adapted(frozen_keys, low_blocks[:, :, 1], upk_blocks)
    value_row_block = adapted(frozen_values, low_blocks[:, :, 2], upv_blocks)
    grad_query, key_gradient, value_gradient = attention_grads(
        query_row_block.reshape(row_count, query_heads, head_size),
        key_row_block.reshape(row_count, kv_heads, head_size),
        value_row_block.reshape(row_count, kv_heads, head_size),
        attention_output_gradient.reshape(row_count, query_heads, head_size),
        document_numbers,
    )
    gq_blocks = grad_query.reshape(block_count, block_rows, -1)
    gk_blocks = key_gradient.reshape(block_count, block_rows, -1)
    gv_blocks = value_gradient.reshape(block_count, block_rows, -1)
    gradient_portion = ADAPTER_SCALE * jnp.concatenate(
        [
            jnp.einsum("brc,bkc->brk", gq_blocks, upq_blocks, precision=PRECISION_HIGH),
            jnp.einsum("brc,bkc->brk", gk_blocks, upk_blocks, precision=PRECISION_HIGH),
            jnp.einsum("brc,bkc->brk", gv_blocks, upv_blocks, precision=PRECISION_HIGH),
        ],
        axis=-1,
    )
    lowrank_grad = lax.psum(gradient_portion.reshape(row_count, 3 * adapter_rank), "mp")
    lowrank_gradient = lowrank_grad.reshape(block_count, block_rows, 3 * adapter_rank)
    down_terms = jnp.einsum("bri,brj->bij", row_blocks, lowrank_gradient, precision=PRECISION_HIGH)
    query_up_terms = ADAPTER_SCALE * jnp.einsum(
        "brk,brc->bkc", low_blocks[:, :, 0], gq_blocks, precision=PRECISION_HIGH
    )
    key_up_terms = ADAPTER_SCALE * jnp.einsum(
        "brk,brc->bkc", low_blocks[:, :, 1], gk_blocks, precision=PRECISION_HIGH
    )
    value_up_terms = ADAPTER_SCALE * jnp.einsum(
        "brk,brc->bkc", low_blocks[:, :, 2], gv_blocks, precision=PRECISION_HIGH
    )
    upkv_terms = jnp.concatenate(
        [
            key_up_terms.reshape(block_count, adapter_rank, kv_heads, head_size),
            value_up_terms.reshape(block_count, adapter_rank, kv_heads, head_size),
        ],
        axis=-1,
    )
    all_slots = lax.all_gather(block_tenant_slot, "dp", axis=0, tiled=True)
    senders = jnp.arange(dp_count * block_count, dtype=jnp.int32) // block_count
    owners = shard_tenant_table[senders, all_slots]
    down_in, upq_in, upkv_in = (
        lax.all_to_all(down_terms, "dp", split_axis=1, concat_axis=0, tiled=True),
        lax.all_to_all(query_up_terms, "dp", split_axis=1, concat_axis=0, tiled=True),
        lax.all_to_all(upkv_terms, "dp", split_axis=1, concat_axis=0, tiled=True),
    )
    owner_hot = (jnp.arange(count_of_tenants, dtype=jnp.int32)[:, None] == owners[None, :]).astype(
        jnp.float32
    )
    grad_down = jnp.einsum("tj,jrc->trc", owner_hot, down_in, precision=PRECISION_HIGH)
    grad_upq = jnp.einsum("tj,jrc->trc", owner_hot, upq_in, precision=PRECISION_HIGH)
    grad_upkv = jnp.einsum("tj,jrkc->trkc", owner_hot, upkv_in, precision=PRECISION_HIGH)
    return (grad_down, grad_upq, grad_upkv)


def solution(mesh):
    placed = (
        P("dp", "mp"),
        P("dp", "mp"),
        P("dp", "mp"),
        P("dp", "mp"),
        P("dp", "mp"),
        P(None, ("mp", "dp"), None),
        P(None, "dp", "mp"),
        P(None, "dp", "mp", None),
        P("dp"),
        P("dp"),
        P(),
    )
    return jax.shard_map(
        on_device,
        mesh=mesh,
        in_specs=placed,
        out_specs=(P(None, ("mp", "dp"), None), P(None, "dp", "mp"), P(None, "dp", "mp", None)),
        check_vma=False,
    )
```

profile of v0, /device:TPU:68, one launch (start us, length us, event | category | flops | bytes accessed | tf_op | source)
XLA Modules:
  0.0 654.9 jit_solution(5255772222505822899)
XLA Ops:
  10.6 17.7 %all-to-all-start.1 = ((f32[128,1,1,256]{3,2,1,0:T(1,128)}), f32[128,1,1,256]{3,2,1,0:T(1,128)S(1)}, u32[]{:S(2)}, u32[]{:S(2)}) async-start(f32[128,1,1,256]{3,2,1,0:T(1,128)} %copy.147), calls=%async_computation.1 | async-start | bytes 262144 | tf_op jit(solution)/shard_map/all_to_all | solution.py:79
  28.3 2.1 gather_fusion.1
  30.5 12.2 %all-to-all-done.1 = f32[128,1,1,256]{3,2,1,0:T(1,128)S(1)} async-done(((f32[128,1,1,256]{3,2,1,0:T(1,128)}), f32[128,1,1,256]{3,2,1,0:T(1,128)S(1)}, u32[]{:S(2)}, u32[]{:S(2)}) %all-to-all-start.1) | async-done | bytes 131104 | tf_op jit(solution)/shard_map/all_to_all | solution.py:79
  42.7 8.8 %all-to-all-start = ((f32[128,16,192]{2,1,0:T(8,128)}), f32[128,16,192]{2,1,0:T(8,128)S(1)}, u32[]{:S(2)}, u32[]{:S(2)}) async-start(f32[128,16,192]{2,1,0:T(8,128)} %gather_fusion.1), calls=%async_computation | async-start | bytes 4194304 | tf_op jit(solution)/shard_map/all_to_all | solution.py:73
  53.7 93.1 %all-to-all-done = f32[128,16,192]{2,1,0:T(8,128)S(1)} async-done(((f32[128,16,192]{2,1,0:T(8,128)}), f32[128,16,192]{2,1,0:T(8,128)S(1)}, u32[]{:S(2)}, u32[]{:S(2)}) %all-to-all-start) | async-done | bytes 1572896 | tf_op jit(solution)/shard_map/all_to_all | solution.py:73
  146.8 11.3 %all-to-all-start.2 = ((f32[128,1,1024]{2,1,0:T(1,128)}), f32[128,1,1024]{2,1,0:T(1,128)}, u32[]{:S(2)}, u32[]{:S(2)}) async-start(f32[128,1,1024]{2,1,0:T(1,128)} %copy.149), calls=%async_computation.2 | async-start | bytes 1048576 | tf_op jit(solution)/shard_map/all_to_all | solution.py:76
  159.9 2.0 copy.145
  161.9 2.1 gather_fusion.2
  164.1 2.9 fusion.45
  168.5 19.0 %all-to-all-done.2 = f32[128,1,1024]{2,1,0:T(1,128)} async-done(((f32[128,1,1024]{2,1,0:T(1,128)}), f32[128,1,1024]{2,1,0:T(1,128)}, u32[]{:S(2)}, u32[]{:S(2)}) %all-to-all-start.2) | async-done | bytes 524320 | tf_op jit(solution)/shard_map/all_to_all | solution.py:76
  189.3 69.0 %all-reduce.4.cloned.1.call-done = f32[3,128,3,64]{1,3,0,2:T(8,128)} async-done(((f32[3,128,3,64]{1,3,0,2:T(8,128)}), f32[3,128,3,64]{1,3,0,2:T(8,128)}) %all-reduce.4.cloned.1.call-update) | async-done | bytes 294928 | tf_op jit(solution)/shard_map/psum | solution.py:88
  259.7 2.3 convolution_multiply_fusion
  265.8 2.0 fusion.10
  267.7 1.6 fusion
  269.4 1.6 fusion.9
  271.0 2.9 copy.157
  274.1 2.3 convolution_bitcast_fusion.3
  279.9 15.7 %all-to-all-start.5 = ((f32[3,64,1,256]{3,2,0,1:T(1,128)}), f32[3,64,1,256]{3,2,0,1:T(1,128)}, u32[]{:S(2)}, u32[]{:S(2)}) async-start(f32[3,64,1,256]{3,2,0,1:T(1,128)} %copy.168), calls=%async_computation.5 | async-start | bytes 393216 | tf_op jit(solution)/shard_map/all_to_all | solution.py:147
  295.6 1.8 convolution_bitcast_fusion.1
  297.4 3.0 copy.155
  302.0 1.9 convolution_multiply_fusion.1
  305.4 6.7 %all-to-all-done.5 = f32[3,64,1,256]{3,2,0,1:T(1,128)} async-done(((f32[3,64,1,256]{3,2,0,1:T(1,128)}), f32[3,64,1,256]{3,2,0,1:T(1,128)}, u32[]{:S(2)}, u32[]{:S(2)}) %all-to-all-start.5) | async-done | bytes 196640 | tf_op jit(solution)/shard_map/all_to_all | solution.py:147
  312.1 9.5 %all-to-all-start.4 = ((f32[3,64,1024]{2,0,1:T(4,128)}), f32[3,64,1024]{2,0,1:T(4,128)}, u32[]{:S(2)}, u32[]{:S(2)}) async-start(f32[3,64,1024]{2,0,1:T(4,128)} %copy.167), calls=%async_computation.4 | async-start | bytes 2097152 | tf_op jit(solution)/shard_map/all_to_all | solution.py:146
  321.6 1.8 convolution_bitcast_fusion.6
  325.2 89.0 %all-reduce.6.cloned.1.call-done = f32[3,128,192]{1,2,0:T(8,128)} async-done(((f32[3,128,192]{1,2,0:T(8,128)}), f32[3,128,192]{1,2,0:T(8,128)}) %all-reduce.6.cloned.1.call-update) | async-done | bytes 294928 | tf_op jit(solution)/shard_map/psum | solution.py:122
  414.3 2.3 convolution_bitcast_fusion
  416.6 3.2 copy.163
  419.8 15.8 %all-to-all-start.3 = ((f32[3,1024,192]{2,0,1:T(4,128)}), f32[3,1024,192]{2,0,1:T(4,128)}, u32[]{:S(2)}, u32[]{:S(2)}) async-start(f32[3,1024,192]{2,0,1:T(4,128)} %copy.163), calls=%async_computation.3 | async-start | bytes 8388608 | tf_op jit(solution)/shard_map/all_to_all | solution.py:145
  437.8 195.0 %all-reduce = s32[192]{0:T(256)S(1)} all-reduce(s32[192]{0:T(256)S(1)} %dynamic-update-slice), channel_id=1, replica_groups=mesh['dp'=64,'mp'=8] {'dp'}, use_global_device_ids=true, to_apply=%add | all-reduce | flops 192 | bytes 1536
  632.9 2.2 gather_fusion
  640.2 2.8 copy.164
  643.3 3.1 fusion.7
  (92 shorter events, 32.7 us)
Async XLA Ops:
  7.2 21.2 %copy-start = (f32[64,16,192]{2,1,0:T(8,128)S(1)}, f32[64,16,192]{2,1,0:T(8,128)}, u32[]{:S(2)}) copy-start(f32[64,16,192]{2,1,0:T(8,128)} %param.16) | copy-start | bytes 2359300
  10.6 32.1 %all-to-all-start.1 = ((f32[128,1,1,256]{3,2,1,0:T(1,128)}), f32[128,1,1,256]{3,2,1,0:T(1,128)S(1)}, u32[]{:S(2)}, u32[]{:S(2)}) async-start(f32[128,1,1,256]{3,2,1,0:T(1,128)} %copy.147), calls=%async_computation.1 | async-start | bytes 262144 | tf_op jit(solution)/shard_map/all_to_all | solution.py:79
  28.3 23.2 %copy-start.10 = (f32[64,1,1024]{2,1,0:T(1,128)S(1)}, f32[64,1,1024]{2,1,0:T(1,128)}, u32[]{:S(2)}) copy-start(f32[64,1,1024]{2,1,0:T(1,128)} %param.17) | copy-start | bytes 786436
  42.7 104.1 %all-to-all-start = ((f32[128,16,192]{2,1,0:T(8,128)}), f32[128,16,192]{2,1,0:T(8,128)S(1)}, u32[]{:S(2)}, u32[]{:S(2)}) async-start(f32[128,16,192]{2,1,0:T(8,128)} %gather_fusion.1), calls=%async_computation | async-start | bytes 4194304 | tf_op jit(solution)/shard_map/all_to_all | solution.py:73
  51.5 106.9 %copy-start.15 = (s32[3]{0:T(128)S(1)}, s32[3]{0:T(128)}, u32[]{:S(2)}) copy-start(s32[3]{0:T(128)} %param.20) | copy-start | bytes 40
  146.8 40.7 %all-to-all-start.2 = ((f32[128,1,1024]{2,1,0:T(1,128)}), f32[128,1,1024]{2,1,0:T(1,128)}, u32[]{:S(2)}, u32[]{:S(2)}) async-start(f32[128,1,1024]{2,1,0:T(1,128)} %copy.149), calls=%async_computation.2 | async-start | bytes 1048576 | tf_op jit(solution)/shard_map/all_to_all | solution.py:76
  158.1 100.2 %all-reduce.4.cloned.1.call-start = ((), (), s32[]{:S(2)}) async-start(), calls=%async_computation.6 | async-start | bytes 589824 | tf_op jit(solution)/shard_map/psum | solution.py:88
  159.9 4.1 copy-start.5
  161.9 5.8 copy-start.13
  164.1 95.6 %copy-start.11 = (bf16[384,128]{1,0:T(8,128)(2,1)S(1)}, bf16[384,128]{1,0:T(8,128)(2,1)}, u32[]{:S(2)}) copy-start(bf16[384,128]{1,0:T(8,128)(2,1)} %param.13) | copy-start | bytes 294916
  167.0 95.1 %copy-start.9 = (bf16[384,1024]{1,0:T(8,128)(2,1)S(1)}, bf16[384,1024]{1,0:T(8,128)(2,1)}, u32[]{:S(2)}) copy-start(bf16[384,1024]{1,0:T(8,128)(2,1)} %param.12) | copy-start | bytes 2359300
  168.5 95.8 %copy-start.6 = (f32[3,64,256]{2,1,0:T(8,128)}, f32[3,64,256]{2,1,0:T(8,128)S(1)}, u32[]{:S(2)}) copy-start(f32[3,64,256]{2,1,0:T(8,128)S(1)} %gather_fusion.4) | copy-start | bytes 589828
  189.3 70.4 %copy-start.3 = (f32[3,64,1024]{2,1,0:T(8,128)}, f32[3,64,1024]{2,1,0:T(8,128)S(1)}, u32[]{:S(2)}) copy-start(f32[3,64,1024]{2,1,0:T(8,128)S(1)} %gather_fusion.6) | copy-start | bytes 2359300
  262.4 3.3 copy-start.12
  263.3 2.4 copy-start.14
  279.9 32.2 %all-to-all-start.5 = ((f32[3,64,1,256]{3,2,0,1:T(1,128)}), f32[3,64,1,256]{3,2,0,1:T(1,128)}, u32[]{:S(2)}, u32[]{:S(2)}) async-start(f32[3,64,1,256]{3,2,0,1:T(1,128)} %copy.168), calls=%async_computation.5 | async-start | bytes 393216 | tf_op jit(solution)/shard_map/all_to_all | solution.py:147
  300.4 21.3 %copy-start.4 = (f32[3,64,1024]{2,1,0:T(8,128)S(1)}, f32[3,64,1024]{2,1,0:T(8,128)}, u32[]{:S(2)}) copy-start(f32[3,64,1024]{2,1,0:T(8,128)} %copy-done.3) | copy-start | bytes 2359300
  302.0 21.5 %copy-start.7 = (f32[3,64,256]{2,1,0:T(8,128)S(1)}, f32[3,64,256]{2,1,0:T(8,128)}, u32[]{:S(2)}) copy-start(f32[3,64,256]{2,1,0:T(8,128)} %copy-done.6) | copy-start | bytes 589828
  302.0 22.0 %copy-start.8 = (f32[384,128,1]{1,0,2:T(8,128)S(1)}, f32[384,128,1]{1,0,2:T(8,128)}, u32[]{:S(2)}) copy-start(f32[384,128,1]{1,0,2:T(8,128)} %fusion.10) | copy-start | bytes 589828
  312.1 107.7 %all-to-all-start.4 = ((f32[3,64,1024]{2,0,1:T(4,128)}), f32[3,64,1024]{2,0,1:T(4,128)}, u32[]{:S(2)}, u32[]{:S(2)}) async-start(f32[3,64,1024]{2,0,1:T(4,128)} %copy.167), calls=%async_computation.4 | async-start | bytes 2097152 | tf_op jit(solution)/shard_map/all_to_all | solution.py:146
  321.6 92.7 %all-reduce.6.cloned.1.call-start = ((), (), s32[]{:S(2)}) async-start(), calls=%async_computation.7 | async-start | bytes 589824 | tf_op jit(solution)/shard_map/psum | solution.py:122
  419.8 213.1 %copy-start.2 = (s32[64,2]{0,1:T(2,128)S(1)}, s32[64,2]{0,1:T(2,128)}, u32[]{:S(2)}) copy-start(s32[64,2]{0,1:T(2,128)} %param.21) | copy-start | bytes 1540
  419.8 220.4 %all-to-all-start.3 = ((f32[3,1024,192]{2,0,1:T(4,128)}), f32[3,1024,192]{2,0,1:T(4,128)}, u32[]{:S(2)}, u32[]{:S(2)}) async-start(f32[3,1024,192]{2,0,1:T(4,128)} %copy.163), calls=%async_computation.3 | async-start | bytes 8388608 | tf_op jit(solution)/shard_map/all_to_all | solution.py:145
  643.0 5.1 copy-start.1
Sparse Core Ops, SparseCore 0:
  167.9 90.3 all-reduce.3
  325.6 88.6 all-reduce.5
where the time goes:
time: 656 us; the launch traced here: 655 us
  waiting for transfers between devices  289 us (44%)
  blocking collectives  195 us (30%)
  starting transfers between devices  79.1 us (12%)
  local copies, waits for them, and re-layouts  42.8 us (7%)
  matrix products  29.8 us (5%)
  between operations  15.3 us (2%)
    unnamed x1, blocking collectives  195 us
    all_to_all x1, waiting for transfers between devices, on_device(): lax.all_to_all(adapter_down_weight[desired_result], 'dp', split_axis=0, c...  93.1 us
    psum x1, waiting for transfers between devices, on_device(): lax.psum(gradient_portion.reshape(row_count, 3 * adapter_rank), 'mp')  89 us
    psum x1, waiting for transfers between devices, on_device(): lowrank = lax.psum(partial_down.reshape(row_count, 3 * adapter_rank), 'mp')  69 us
    all_to_all x1, waiting for transfers between devices, on_device(): lax.all_to_all(adapter_up_query[desired_result], 'dp', split_axis=0, conc...  19 us
    all_to_all x1, starting transfers between devices, on_device(): lax.all_to_all(adapter_up_key_value[desired_result], 'dp', split_axis=0,...  17.7 us
    all_to_all x1, starting transfers between devices, on_device(): lax.all_to_all(down_terms, 'dp', split_axis=1, concat_axis=0, tiled=True)  15.8 us
    all_to_all x1, starting transfers between devices, on_device(): lax.all_to_all(upkv_terms, 'dp', split_axis=1, concat_axis=0, tiled=True)  15.7 us
  transfers between devices with their start and end apart: 8, of which 6 were waited for; matrix products, arithmetic and copies ran while one was open for 7% of the time, Pallas kernels for 0%

commit v1 on v0

--- a/solution.py
+++ b/solution.py
@@ -119,7 +119,9 @@
         ],
         axis=-1,
     )
-    lowrank_grad = lax.psum(gradient_portion.reshape(row_count, 3 * adapter_rank), "mp")
+    lowrank_grad = jnp.sum(
+        lax.all_gather(gradient_portion.reshape(row_count, 3 * adapter_rank), "mp"), axis=0
+    )
     lowrank_gradient = lowrank_grad.reshape(block_count, block_rows, 3 * adapter_rank)
     down_terms = jnp.einsum("bri,brj->bij", row_blocks, lowrank_gradient, precision=PRECISION_HIGH)
     query_up_terms = ADAPTER_SCALE * jnp.einsum(

time: 656 us -> 608 us (0.927)
  waiting for transfers between devices: 289 us -> 251 us
    psum x1 -> x0, waiting for transfers between devices: 89 us -> none  [on_device(): lax.psum(gradient_portion.reshape(row_count, 3 * adapter_rank), 'mp')]
    all_to_all x1, waiting for transfers between devices: 0.01 us -> 37.8 us  [on_device(): lax.all_to_all(query_up_terms, 'dp', split_axis=1, concat_axis=0, tiled=T...]
    all_to_all x1, waiting for transfers between devices: 6.69 us -> 14.1 us  [on_device(): lax.all_to_all(upkv_terms, 'dp', split_axis=1, concat_axis=0, tiled=True)]
  transfers between devices with their start and end apart: 8 -> 8, of which waited for: 6 -> 7; matrix products, arithmetic and copies ran while one was open for 7% -> 6% of each run, Pallas kernels for 0% -> 0%
where the time goes in v1:
time: 608 us; the launch traced here: 607 us
  waiting for transfers between devices  251 us (41%)
  blocking collectives  195 us (32%)
  starting transfers between devices  73.4 us (12%)
  local copies, waits for them, and re-layouts  41.3 us (7%)
  matrix products  25.1 us (4%)
  between operations  15.3 us (3%)
  other arithmetic  6.37 us (1%)
    unnamed x1, blocking collectives  195 us
    all_to_all x1, waiting for transfers between devices, on_device(): lax.all_to_all(adapter_down_weight[desired_result], 'dp', split_axis=0, c...  93.1 us
    psum x1, waiting for transfers between devices, on_device(): lowrank = lax.psum(partial_down.reshape(row_count, 3 * adapter_rank), 'mp')  68.7 us
    all_to_all x1, waiting for transfers between devices, on_device(): lax.all_to_all(query_up_terms, 'dp', split_axis=1, concat_axis=0, tiled=T...  37.8 us
    all_to_all x1, waiting for transfers between devices, on_device(): lax.all_to_all(adapter_up_query[desired_result], 'dp', split_axis=0, conc...  19 us
    all_to_all x1, starting transfers between devices, on_device(): lax.all_to_all(adapter_up_key_value[desired_result], 'dp', split_axis=0,...  17.7 us
    all_to_all x1, starting transfers between devices, on_device(): lax.all_to_all(upkv_terms, 'dp', split_axis=1, concat_axis=0, tiled=True)  15.5 us
    all_to_all x1, waiting for transfers between devices, on_device(): lax.all_to_all(upkv_terms, 'dp', split_axis=1, concat_axis=0, tiled=True)  14.1 us
  transfers between devices with their start and end apart: 8, of which 7 were waited for; matrix products, arithmetic and copies ran while one was open for 6% of the time, Pallas kernels for 0%

profile of v1, /device:TPU:68, one launch (start us, length us, event | category | flops | bytes accessed | tf_op | source)
XLA Modules:
  0.0 607.1 jit_solution(10726870892923768372)
XLA Ops:
  10.6 17.7 %all-to-all-start.1 = ((f32[128,1,1,256]{3,2,1,0:T(1,128)}), f32[128,1,1,256]{3,2,1,0:T(1,128)S(1)}, u32[]{:S(2)}, u32[]{:S(2)}) async-start(f32[128,1,1,256]{3,2,1,0:T(1,128)} %copy.147), calls=%async_computation.1 | async-start | bytes 262144 | tf_op jit(solution)/shard_map/all_to_all | solution.py:79
  28.3 2.1 gather_fusion.1
  30.4 12.3 %all-to-all-done.1 = f32[128,1,1,256]{3,2,1,0:T(1,128)S(1)} async-done(((f32[128,1,1,256]{3,2,1,0:T(1,128)}), f32[128,1,1,256]{3,2,1,0:T(1,128)S(1)}, u32[]{:S(2)}, u32[]{:S(2)}) %all-to-all-start.1) | async-done | bytes 131104 | tf_op jit(solution)/shard_map/all_to_all | solution.py:79
  42.7 8.8 %all-to-all-start = ((f32[128,16,192]{2,1,0:T(8,128)}), f32[128,16,192]{2,1,0:T(8,128)S(1)}, u32[]{:S(2)}, u32[]{:S(2)}) async-start(f32[128,16,192]{2,1,0:T(8,128)} %gather_fusion.1), calls=%async_computation | async-start | bytes 4194304 | tf_op jit(solution)/shard_map/all_to_all | solution.py:73
  53.7 93.1 %all-to-all-done = f32[128,16,192]{2,1,0:T(8,128)S(1)} async-done(((f32[128,16,192]{2,1,0:T(8,128)}), f32[128,16,192]{2,1,0:T(8,128)S(1)}, u32[]{:S(2)}, u32[]{:S(2)}) %all-to-all-start) | async-done | bytes 1572896 | tf_op jit(solution)/shard_map/all_to_all | solution.py:73
  146.8 11.3 %all-to-all-start.2 = ((f32[128,1,1024]{2,1,0:T(1,128)}), f32[128,1,1024]{2,1,0:T(1,128)}, u32[]{:S(2)}, u32[]{:S(2)}) async-start(f32[128,1,1024]{2,1,0:T(1,128)} %copy.149), calls=%async_computation.2 | async-start | bytes 1048576 | tf_op jit(solution)/shard_map/all_to_all | solution.py:76
  159.8 1.9 copy.145
  161.7 2.1 gather_fusion.2
  163.8 2.9 fusion.48
  168.5 19.0 %all-to-all-done.2 = f32[128,1,1024]{2,1,0:T(1,128)} async-done(((f32[128,1,1024]{2,1,0:T(1,128)}), f32[128,1,1024]{2,1,0:T(1,128)}, u32[]{:S(2)}, u32[]{:S(2)}) %all-to-all-start.2) | async-done | bytes 524320 | tf_op jit(solution)/shard_map/all_to_all | solution.py:76
  189.3 68.7 %all-reduce.3.cloned.1.call-done = f32[3,128,3,64]{1,3,0,2:T(8,128)} async-done(((f32[3,128,3,64]{1,3,0,2:T(8,128)}), f32[3,128,3,64]{1,3,0,2:T(8,128)}) %all-reduce.3.cloned.1.call-update) | async-done | bytes 294928 | tf_op jit(solution)/shard_map/psum | solution.py:88
  259.5 2.3 convolution_multiply_fusion
  265.5 2.0 fusion.10
  267.5 1.7 fusion
  269.2 1.6 fusion.9
  270.8 3.2 copy.157
  273.9 1.7 convolution_bitcast_fusion.1
  277.1 1.6 copy.155
  280.4 1.8 fusion.49
  285.9 15.5 %all-to-all-start.5 = ((f32[3,64,1,256]{3,2,0,1:T(1,128)}), f32[3,64,1,256]{3,2,0,1:T(1,128)S(1)}, u32[]{:S(2)}, u32[]{:S(2)}) async-start(f32[3,64,1,256]{3,2,0,1:T(1,128)} %copy.168), calls=%async_computation.5 | async-start | bytes 393216 | tf_op jit(solution)/shard_map/all_to_all | solution.py:149
  303.9 14.1 %all-to-all-done.5 = f32[3,64,1,256]{3,2,0,1:T(1,128)S(1)} async-done(((f32[3,64,1,256]{3,2,0,1:T(1,128)}), f32[3,64,1,256]{3,2,0,1:T(1,128)S(1)}, u32[]{:S(2)}, u32[]{:S(2)}) %all-to-all-start.5) | async-done | bytes 196640 | tf_op jit(solution)/shard_map/all_to_all | solution.py:149
  318.0 9.4 %all-to-all-start.4 = ((f32[3,64,1024]{2,0,1:T(4,128)}), f32[3,64,1024]{2,0,1:T(4,128)}, u32[]{:S(2)}, u32[]{:S(2)}) async-start(f32[3,64,1024]{2,0,1:T(4,128)} %copy.167), calls=%async_computation.4 | async-start | bytes 2097152 | tf_op jit(solution)/shard_map/all_to_all | solution.py:148
  327.5 5.6 all-gather.2.cloned.1.call-done
  333.1 2.5 reduce_sum.29
  335.6 2.0 convolution_bitcast_fusion
  337.7 3.2 copy.163
  340.9 37.8 %all-to-all-done.4 = f32[3,64,1024]{2,0,1:T(4,128)} async-done(((f32[3,64,1024]{2,0,1:T(4,128)}), f32[3,64,1024]{2,0,1:T(4,128)}, u32[]{:S(2)}, u32[]{:S(2)}) %all-to-all-start.4) | async-done | bytes 786464 | tf_op jit(solution)/shard_map/all_to_all | solution.py:148
  378.6 10.4 %all-to-all-start.3 = ((f32[3,1024,192]{2,0,1:T(4,128)}), f32[3,1024,192]{2,0,1:T(4,128)}, u32[]{:S(2)}, u32[]{:S(2)}) async-start(f32[3,1024,192]{2,0,1:T(4,128)} %copy.163), calls=%async_computation.3 | async-start | bytes 8388608 | tf_op jit(solution)/shard_map/all_to_all | solution.py:147
  391.2 195.0 %all-reduce = s32[192]{0:T(256)S(1)} all-reduce(s32[192]{0:T(256)S(1)} %dynamic-update-slice), channel_id=1, replica_groups=mesh['dp'=64,'mp'=8] {'dp'}, use_global_device_ids=true, to_apply=%add | all-reduce | flops 192 | bytes 1536
  586.3 2.0 gather_fusion
  592.4 2.8 copy.164
  595.5 3.1 fusion.7
  (105 shorter events, 32.3 us)
Async XLA Ops:
  7.2 21.2 %copy-start = (f32[64,16,192]{2,1,0:T(8,128)S(1)}, f32[64,16,192]{2,1,0:T(8,128)}, u32[]{:S(2)}) copy-start(f32[64,16,192]{2,1,0:T(8,128)} %param.16) | copy-start | bytes 2359300
  10.6 32.1 %all-to-all-start.1 = ((f32[128,1,1,256]{3,2,1,0:T(1,128)}), f32[128,1,1,256]{3,2,1,0:T(1,128)S(1)}, u32[]{:S(2)}, u32[]{:S(2)}) async-start(f32[128,1,1,256]{3,2,1,0:T(1,128)} %copy.147), calls=%async_computation.1 | async-start | bytes 262144 | tf_op jit(solution)/shard_map/all_to_all | solution.py:79
  30.4 21.1 %copy-start.14 = (f32[64,1,1024]{2,1,0:T(1,128)S(1)}, f32[64,1,1024]{2,1,0:T(1,128)}, u32[]{:S(2)}) copy-start(f32[64,1,1024]{2,1,0:T(1,128)} %param.17) | copy-start | bytes 786436
  42.7 104.1 %all-to-all-start = ((f32[128,16,192]{2,1,0:T(8,128)}), f32[128,16,192]{2,1,0:T(8,128)S(1)}, u32[]{:S(2)}, u32[]{:S(2)}) async-start(f32[128,16,192]{2,1,0:T(8,128)} %gather_fusion.1), calls=%async_computation | async-start | bytes 4194304 | tf_op jit(solution)/shard_map/all_to_all | solution.py:73
  51.6 106.6 %copy-start.19 = (s32[3]{0:T(128)S(1)}, s32[3]{0:T(128)}, u32[]{:S(2)}) copy-start(s32[3]{0:T(128)} %param.20) | copy-start | bytes 40
  146.8 40.7 %all-to-all-start.2 = ((f32[128,1,1024]{2,1,0:T(1,128)}), f32[128,1,1024]{2,1,0:T(1,128)}, u32[]{:S(2)}, u32[]{:S(2)}) async-start(f32[128,1,1024]{2,1,0:T(1,128)} %copy.149), calls=%async_computation.2 | async-start | bytes 1048576 | tf_op jit(solution)/shard_map/all_to_all | solution.py:76
  158.1 99.9 %all-reduce.3.cloned.1.call-start = ((), (), s32[]{:S(2)}) async-start(), calls=%async_computation.6 | async-start | bytes 589824 | tf_op jit(solution)/shard_map/psum | solution.py:88
  161.6 2.2 copy-start.7
  163.8 3.9 copy-start.17
  166.7 92.7 %copy-start.15 = (bf16[384,128]{1,0:T(8,128)(2,1)S(1)}, bf16[384,128]{1,0:T(8,128)(2,1)}, u32[]{:S(2)}) copy-start(bf16[384,128]{1,0:T(8,128)(2,1)} %param.13) | copy-start | bytes 294916
  167.5 165.6 %all-gather.2.cloned.1.call-start = ((), (), s32[]{:S(2)}) async-start(), calls=%async_computation.7 | async-start | bytes 2654208 | tf_op jit(solution)/shard_map/all_gather | solution.py:123
  167.9 93.9 %copy-start.13 = (bf16[384,1024]{1,0:T(8,128)(2,1)S(1)}, bf16[384,1024]{1,0:T(8,128)(2,1)}, u32[]{:S(2)}) copy-start(bf16[384,1024]{1,0:T(8,128)(2,1)} %param.12) | copy-start | bytes 2359300
  168.5 95.6 %copy-start.9 = (f32[3,64,256]{2,1,0:T(8,128)}, f32[3,64,256]{2,1,0:T(8,128)S(1)}, u32[]{:S(2)}) copy-start(f32[3,64,256]{2,1,0:T(8,128)S(1)} %gather_fusion.4) | copy-start | bytes 589828
  189.3 70.2 %copy-start.4 = (f32[3,64,1024]{2,1,0:T(8,128)}, f32[3,64,1024]{2,1,0:T(8,128)S(1)}, u32[]{:S(2)}) copy-start(f32[3,64,1024]{2,1,0:T(8,128)S(1)} %gather_fusion.6) | copy-start | bytes 2359300
  263.0 2.4 copy-start.16
  263.0 2.4 copy-start.18
  273.9 1.9 copy-start.3
  275.7 1.4 copy-start.6
  277.1 3.2 copy-start.5
  278.8 3.5 copy-start.10
  278.8 4.2 copy-start.12
  280.4 4.0 copy-start.11
  285.9 32.1 %all-to-all-start.5 = ((f32[3,64,1,256]{3,2,0,1:T(1,128)}), f32[3,64,1,256]{3,2,0,1:T(1,128)S(1)}, u32[]{:S(2)}, u32[]{:S(2)}) async-start(f32[3,64,1,256]{3,2,0,1:T(1,128)} %copy.168), calls=%async_computation.5 | async-start | bytes 393216 | tf_op jit(solution)/shard_map/all_to_all | solution.py:149
  303.9 31.7 %copy-start.8 = (bf16[384,1024]{1,0:T(8,128)(2,1)S(1)}, bf16[384,1024]{1,0:T(8,128)(2,1)}, u32[]{:S(2)}) copy-start(bf16[384,1024]{1,0:T(8,128)(2,1)} %param.11) | copy-start | bytes 2359300
  318.0 60.6 %all-to-all-start.4 = ((f32[3,64,1024]{2,0,1:T(4,128)}), f32[3,64,1024]{2,0,1:T(4,128)}, u32[]{:S(2)}, u32[]{:S(2)}) async-start(f32[3,64,1024]{2,0,1:T(4,128)} %copy.167), calls=%async_computation.4 | async-start | bytes 2097152 | tf_op jit(solution)/shard_map/all_to_all | solution.py:148
  340.9 245.4 %copy-start.2 = (s32[64,2]{0,1:T(2,128)S(1)}, s32[64,2]{0,1:T(2,128)}, u32[]{:S(2)}) copy-start(s32[64,2]{0,1:T(2,128)} %param.21) | copy-start | bytes 1540
  378.6 213.8 %all-to-all-start.3 = ((f32[3,1024,192]{2,0,1:T(4,128)}), f32[3,1024,192]{2,0,1:T(4,128)}, u32[]{:S(2)}, u32[]{:S(2)}) async-start(f32[3,1024,192]{2,0,1:T(4,128)} %copy.163), calls=%async_computation.3 | async-start | bytes 8388608 | tf_op jit(solution)/shard_map/all_to_all | solution.py:147
  595.5 4.8 copy-start.1
Sparse Core Ops, SparseCore 0:
  167.6 90.3 all-reduce.2
  284.5 48.5 all-gather.1
